TPU v7x, 128 devices: a whole 4x4x4 slice. The times are simulated.
128 devices in a mesh: row: 4 (over z), col: 16 (over x_hi, y, core), smp: 2 (over x_lo).
Axes of the slice: x: 4 (x_hi: 2, x_lo: 2; x = x_hi * 2 + x_lo), y: 4, z: 4, core: 2. Of those that a mesh axis runs over, the one named last changes fastest.
Arguments:
- pair_repr: bfloat16 [512, 512, 128], P('row', 'col'), may hold values from -6 to 6
- tri_weight: bfloat16 [128, 512], replicated, may hold values from -0.75 to 0.75
- tri_bias_weight: bfloat16 [128, 4], replicated, may hold values from -40 to 40
- tri_output_weight: bfloat16 [128, 128], replicated, may hold values from -0.5 to 0.5
- samples: bfloat16 [8, 512, 768], P('smp'), may hold values from -6 to 6
- levels: int32 [8], P('smp'), may hold values from 0 to 199
- single_cond: bfloat16 [512, 384], replicated, may hold values from -6 to 6
- noise_weight: bfloat16 [256, 384], replicated, may hold values from -0.375 to 0.375
- modulation_weight: bfloat16 [384, 1536], replicated, may hold values from -0.3125 to 0.3125
- attention_weight: bfloat16 [768, 3072], replicated, may hold values from -0.5 to 0.5
- pair_bias_weight: bfloat16 [128, 16], replicated, may hold values from -40 to 40
- output_weight: bfloat16 [768, 768], replicated, may hold values from -0.21875 to 0.21875
- output_gate_weight: bfloat16 [384, 768], replicated, may hold values from -0.3125 to 0.3125
Outputs:
- new_pair: bfloat16 [512, 512, 128], P('row', 'col')
- attn_update: bfloat16 [8, 512, 768], P('smp', ('row', 'col'))
All inputs are finite; a program needn't handle non-finite values.
Results may differ from a plain program's by a relative error of at most 0.02.
The roundings to bfloat16 on the way count: a program that leaves them out, or rounds other values in their place, can miss the bound.
Values may be sent and summed in bfloat16 or wider, within the bound.
A program may use at most 128 MiB of HBM per device.

v0:
```python
import math
import jax
import jax.numpy as jnp
from jax import lax
from jax.sharding import PartitionSpec as P

HT = 4
DT = 32
CA = 768
HD = 16
DH = 48
NE = 256
LEVELS = 200
NORM_EPSILON = 1e-05
SIGMA_DATA = 16.0
SIGMA_MAX = 160.0
SIGMA_MIN = 0.0004


def combined_all(part, axis, combine):
    gathered = jax.tree.map(lambda a: lax.all_gather(a, axis), part)

    def take(source):
        return jax.tree.map(lambda a: lax.dynamic_index_in_dim(a, source, 0, False), gathered)

    return lax.fori_loop(
        1, lax.axis_size(axis), lambda source, state: combine(state, take(source)), take(0)
    )


def normalize(values):
    values = values.astype(jnp.float32)
    average = jnp.mean(values, axis=-1, keepdims=True)
    centred = values - average
    variance = jnp.mean(centred * centred, axis=-1, keepdims=True)
    return centred * lax.rsqrt(variance + NORM_EPSILON)


def noise_features(levels):
    fraction = levels.astype(jnp.float32) / (LEVELS - 1)
    upper_root = SIGMA_MAX ** (1.0 / 7.0)
    lower_root = SIGMA_MIN ** (1.0 / 7.0)
    noise_sigma = SIGMA_DATA * (upper_root + fraction * (lower_root - upper_root)) ** 7
    scaled = 0.25 * jnp.log(noise_sigma / SIGMA_DATA)
    frequency = (
        2.0
        * math.pi
        * jnp.exp(jnp.arange(NE // 2, dtype=jnp.float32) * (math.log(100.0) / (NE // 2)))
    )
    angles = scaled[:, None] * frequency[None, :]
    return jnp.concatenate([jnp.cos(angles), jnp.sin(angles)], axis=-1)


def attend_columns(pair_cols, bias_full, tri_weight, tri_output_weight):
    row_count, col_count, channels = pair_cols.shape
    normed = normalize(pair_cols).astype(jnp.bfloat16)
    projected = jnp.dot(
        normed.reshape(row_count * col_count, channels),
        tri_weight,
        preferred_element_type=jnp.float32,
    )
    projected = projected.reshape(row_count, col_count, 4, HT * DT)
    query_part = (projected[:, :, 0] * DT ** (-0.5)).astype(jnp.bfloat16)
    key_part = projected[:, :, 1].astype(jnp.bfloat16)
    value_part = projected[:, :, 2].astype(jnp.bfloat16)
    gate_part = projected[:, :, 3]

    def one_column(column):
        query_col = lax.dynamic_index_in_dim(query_part, column, 1, keepdims=False).reshape(
            row_count, HT, DT
        )
        key_col = lax.dynamic_index_in_dim(key_part, column, 1, keepdims=False).reshape(
            row_count, HT, DT
        )
        value_col = lax.dynamic_index_in_dim(value_part, column, 1, keepdims=False).reshape(
            row_count, HT, DT
        )
        gate_col = lax.dynamic_index_in_dim(gate_part, column, 1, keepdims=False)
        scores = jnp.einsum("ihd,khd->hik", query_col, key_col, preferred_element_type=jnp.float32)
        scores = scores + bias_full
        row_peak = jnp.max(scores, axis=-1, keepdims=True)
        exponent = jnp.exp(scores - row_peak)
        row_total = jnp.sum(exponent, axis=-1)
        attended = jnp.einsum(
            "hik,khd->ihd",
            exponent.astype(jnp.bfloat16),
            value_col,
            preferred_element_type=jnp.float32,
        )
        attended = attended / jnp.transpose(row_total)[:, :, None]
        return (jax.nn.sigmoid(gate_col) * attended.reshape(row_count, HT * DT)).astype(
            jnp.bfloat16
        )

    gated = lax.map(one_column, jnp.arange(col_count, dtype=jnp.int32))
    update = jnp.einsum("jic,cz->ijz", gated, tri_output_weight, preferred_element_type=jnp.float32)
    return (pair_cols.astype(jnp.float32) + update).astype(jnp.bfloat16)


def combine_parts(first, second):
    peak_one, total_one, sum_one = first
    peak_two, total_two, sum_two = second
    row_peak = jnp.maximum(peak_one, peak_two)
    factor_one = jnp.exp(peak_one - row_peak)
    factor_two = jnp.exp(peak_two - row_peak)
    row_total = total_one * factor_one + total_two * factor_two
    sample_count, token_count, channels = sum_one.shape
    head_count = row_peak.shape[1]

    def rescale(summed, factor):
        shaped = summed.reshape(sample_count, token_count, head_count, channels // head_count)
        return (shaped * jnp.transpose(factor, (0, 2, 1))[..., None]).reshape(
            sample_count, token_count, channels
        )

    return (row_peak, row_total, rescale(sum_one, factor_one) + rescale(sum_two, factor_two))


def local(
    pair_repr,
    tri_weight,
    tri_bias_weight,
    tri_output_weight,
    samples,
    levels,
    single_cond,
    noise_weight,
    modulation_weight,
    attention_weight,
    pair_bias_weight,
    output_weight,
    output_gate_weight,
):
    rows_here, cols_here, channels = pair_repr.shape
    col_count = lax.axis_size("col")
    row_index = lax.axis_index("row")
    col_index = lax.axis_index("col")
    normed_tile = normalize(pair_repr).astype(jnp.bfloat16)
    local_bias = jnp.einsum(
        "kiz,zh->hik", normed_tile, tri_bias_weight, preferred_element_type=jnp.float32
    )
    partial_bias = lax.all_gather(local_bias, "row", axis=2, tiled=True)
    bias_full = lax.all_gather(partial_bias, "col", axis=1, tiled=True)
    columns = lax.all_to_all(pair_repr, "row", split_axis=1, concat_axis=0, tiled=True)
    updated = attend_columns(columns, bias_full, tri_weight, tri_output_weight)
    new_tile = lax.all_to_all(updated, "row", split_axis=0, concat_axis=1, tiled=True)
    sample_count = samples.shape[0]
    own_count = rows_here // col_count
    own_start = col_index * own_count
    query_start = row_index * rows_here
    key_start = col_index * cols_here
    features = noise_features(levels).astype(jnp.bfloat16)
    noise_terms = jnp.dot(features, noise_weight, preferred_element_type=jnp.float32)

    def adapt(start, count):
        trunk = lax.dynamic_slice_in_dim(single_cond, start, count, 0).astype(jnp.float32)
        conditioned = normalize(trunk[None, :, :] + noise_terms[:, None, :]).astype(jnp.bfloat16)
        activation = lax.dynamic_slice_in_dim(samples, start, count, 1)
        modulation = jnp.einsum(
            "stc,cd->std", conditioned, modulation_weight, preferred_element_type=jnp.float32
        )
        adapted = (
            jax.nn.sigmoid(modulation[..., :CA]) * normalize(activation) + modulation[..., CA:]
        ).astype(jnp.bfloat16)
        return (conditioned, adapted)

    pair_renormed = normalize(new_tile).astype(jnp.bfloat16)
    pair_bias = jnp.einsum(
        "ikz,zh->hik", pair_renormed, pair_bias_weight, preferred_element_type=jnp.float32
    )
    cond_rows, adapted_rows = adapt(query_start, rows_here)
    cond_keys, adapted_keys = adapt(key_start, cols_here)
    query_part = jnp.einsum(
        "stc,cd->std", adapted_rows, attention_weight[:, :CA], preferred_element_type=jnp.float32
    )
    query_part = (
        (query_part * DH ** (-0.5)).astype(jnp.bfloat16).reshape(sample_count, rows_here, HD, DH)
    )
    key_value = jnp.einsum(
        "stc,cd->std",
        adapted_keys,
        attention_weight[:, CA : 3 * CA],
        preferred_element_type=jnp.float32,
    )
    key_part = key_value[..., :CA].astype(jnp.bfloat16).reshape(sample_count, cols_here, HD, DH)
    value_part = key_value[..., CA:].astype(jnp.bfloat16).reshape(sample_count, cols_here, HD, DH)
    scores = (
        jnp.einsum("sihd,skhd->shik", query_part, key_part, preferred_element_type=jnp.float32)
        + pair_bias[None]
    )
    adapted_own = lax.dynamic_slice_in_dim(adapted_rows, own_start, own_count, 1)
    cond_own = lax.dynamic_slice_in_dim(cond_rows, own_start, own_count, 1)
    local_peak = jnp.max(scores, axis=-1)
    exponent = jnp.exp(scores - local_peak[..., None])
    local_total = jnp.sum(exponent, axis=-1)
    partial_value = jnp.einsum(
        "shik,skhd->sihd",
        exponent.astype(jnp.bfloat16),
        value_part,
        preferred_element_type=jnp.float32,
    )
    partial_value = partial_value.reshape(sample_count, rows_here, CA)
    row_peak, row_total, summed = combined_all(
        (local_peak, local_total, partial_value), "col", combine_parts
    )
    row_total = lax.dynamic_slice_in_dim(row_total, own_start, own_count, 2)
    summed = lax.dynamic_slice_in_dim(summed, own_start, own_count, 1)
    attended = (
        summed.reshape(sample_count, own_count, HD, DH)
        / jnp.transpose(row_total, (0, 2, 1))[..., None]
    )
    attended = attended.reshape(sample_count, own_count, CA)
    gate_part = jnp.einsum(
        "stc,cd->std",
        adapted_own,
        attention_weight[:, 3 * CA :],
        preferred_element_type=jnp.float32,
    )
    gated = (jax.nn.sigmoid(gate_part) * attended).astype(jnp.bfloat16)
    projected_out = jnp.einsum(
        "stc,cd->std", gated, output_weight, preferred_element_type=jnp.float32
    )
    out_gate = jax.nn.sigmoid(
        jnp.einsum("stc,cd->std", cond_own, output_gate_weight, preferred_element_type=jnp.float32)
    )
    attn_update = (out_gate * projected_out).astype(jnp.bfloat16)
    return (new_tile, attn_update)


def solution(mesh):
    return jax.shard_map(
        local,
        mesh=mesh,
        in_specs=(
            P("row", "col", None),
            P(),
            P(),
            P(),
            P("smp", None, None),
            P("smp"),
            P(),
            P(),
            P(),
            P(),
            P(),
            P(),
            P(),
        ),
        out_specs=(P("row", "col", None), P("smp", ("row", "col"), None)),
        check_vma=False,
    )
```

profile of v0, /device:TPU:1, one launch (start us, length us, event | category | flops | bytes accessed | tf_op | source)
XLA Modules:
  0.0 460.5 jit_solution(10458823537242216250)
XLA Ops:
  13.5 12.3 %all_gather.21 = f32[4,32,512]{2,1,0:T(8,128)S(1)} all-gather(f32[4,32,128]{2,1,0:T(8,128)S(1)} %copy.113), channel_id=1, replica_groups=mesh['row'=4,'col'=16,'smp'=2] {'row'}, dimensions={2}, use_global_device_ids=true | all-gather | bytes 327680 | tf_op jit(solution)/shard_map/all_gather | solution.py:142
  28.1 3.8 all-to-all-start
  55.0 30.4 %all-gather.5.cloned.1.call-done = f32[4,512,512]{2,0,1:T(4,128)} async-done(((f32[4,32,512]{2,0,1:T(4,128)}), f32[4,512,512]{2,0,1:T(4,128)}) %all-gather.5.cloned.1.call-update) | async-done | bytes 4194320 | tf_op jit(solution)/shard_map/all_gather | solution.py:143
  85.4 5.2 %copy.119 = f32[4,512,512]{1,2,0:T(8,128)} copy(f32[4,512,512]{2,0,1:T(4,128)} %all-gather.5.cloned.1.call-done) | data formatting | bytes 8388608 | tf_op jit(solution)/shard_map/while | solution.py:95
  90.7 87.0 %while.29 = (s32[]{:T(128)}, bf16[8,512,128]{1,2,0:T(8,128)(2,1)}, s32[8]{0:T(128)S(1)}, f32[512,8,128]{2,0,1:T(8,128)}, bf16[512,8,128]{2,0,1:T(8,128)(2,1)}, /...) while((s32[]{:T(128)}, bf16[8,512,128]{1,2,0:T(8,128)(2,1)}, ...), condition=%wide.region_7.8_spmd, body=%wide.region_4.7_spmd.sunk | while | flops 140898304 | bytes 20750516 | solution.py:95
  96.6 3.0 fusion.174
  107.4 3.0 fusion.174
  118.3 3.0 fusion.174
  129.2 3.0 fusion.174
  140.1 3.0 fusion.174
  150.9 3.0 fusion.174
  161.8 3.0 fusion.174
  172.7 3.0 fusion.174
  181.1 4.1 all-to-all-start.1
  190.8 2.9 multiply_convert_fusion.2
  195.3 4.6 all-to-all-done.1
  203.2 2.9 convolution_bitcast_fusion
  211.0 24.7 %all-gather = f32[64,16,128]{2,1,0:T(8,128)S(1)} all-gather(f32[4,16,128]{2,1,0:T(8,128)S(1)} %get-tuple-element.335), channel_id=2, replica_groups=mesh['row'=4,'col'=16,'smp'=2] {'col'}, dimensions={0}, use_global_device_ids=true | all-gather | bytes 557056 | tf_op jit(solution)/shard_map/all_gather | solution.py:21
  236.0 22.1 %all-gather.1 = f32[64,16,128]{2,1,0:T(8,128)S(1)} all-gather(f32[4,16,128]{2,1,0:T(8,128)S(1)} %fusion.85), channel_id=3, replica_groups=mesh['row'=4,'col'=16,'smp'=2] {'col'}, dimensions={0}, use_global_device_ids=true | all-gather | bytes 557056 | tf_op jit(solution)/shard_map/all_gather | solution.py:21
  258.1 98.4 %all-gather.7.cloned.1.call-done = f32[16,4,128,768]{3,2,1,0:T(8,128)} async-done(((f32[1,4,128,768]{3,2,1,0:T(8,128)}), f32[16,4,128,768]{3,2,1,0:T(8,128)}) %all-gather.7.cloned.1.call-update) | async-done | bytes 25165840 | tf_op jit(solution)/shard_map/all_gather | solution.py:21
  359.7 88.7 %while.30 = (s32[]{:T(128)}, f32[4,16,128]{2,1,0:T(8,128)S(1)}, f32[4,16,128]{2,1,0:T(8,128)S(1)}, f32[4,128,768]{1,2,0:T(8,128)}, f32[16,4,16,128]{3,2,1,0:T(8,...) while((s32[]{:T(128)}, f32[4,16,128]{2,1,0:T(8,128)S(1)}, ...), condition=%wide.region_21.22_spmd, body=%wide.region_20.21_spmd.sunk | while | flops 1236997 | bytes 19890436 | solution.py:26
  368.7 2.9 fusion.179
  374.6 2.9 fusion.179
  380.5 2.9 fusion.179
  386.4 2.9 fusion.179
  392.3 2.9 fusion.179
  398.2 2.9 fusion.179
  404.1 2.9 fusion.179
  410.0 2.9 fusion.179
  415.9 2.9 fusion.179
  421.9 2.9 fusion.179
  427.8 2.9 fusion.179
  (400 shorter events, 162.6 us)
Async XLA Ops:
  7.2 33.0 %copy-start = (bf16[384,1536]{1,0:T(8,128)(2,1)S(1)}, bf16[384,1536]{1,0:T(8,128)(2,1)}, u32[]{:S(2)}) copy-start(bf16[384,1536]{1,0:T(8,128)(2,1)} %param.25) | copy-start | bytes 3538948
  7.2 4.4 copy-start.2
  7.2 4.4 copy-start.17
  7.2 78.2 %all-gather.5.cloned.1.call-start = ((), (), s32[]{:S(2)}) async-start(), calls=%async_computation.2 | async-start | bytes 4456448 | tf_op jit(solution)/shard_map/all_gather | solution.py:143
  26.7 5.3 %copy-start.13 = (bf16[128,512]{1,0:T(8,128)(2,1)S(1)}, bf16[128,512]{1,0:T(8,128)(2,1)}, u32[]{:S(2)}) copy-start(bf16[128,512]{1,0:T(8,128)(2,1)} %param.18) | copy-start | bytes 393220
  28.1 7.4 %copy-start.18 = (s32[4]{0:T(128)S(1)}, s32[4]{0:T(128)}, u32[]{:S(2)}) copy-start(s32[4]{0:T(128)} %param.22) | copy-start | bytes 52
  28.1 7.6 %copy-start.12 = (bf16[256,384]{1,0:T(8,128)(2,1)S(1)}, bf16[256,384]{1,0:T(8,128)(2,1)}, u32[]{:S(2)}) copy-start(bf16[256,384]{1,0:T(8,128)(2,1)} %param.24) | copy-start | bytes 589828
  28.1 16.9 %all-to-all-start = ((bf16[128,32,128]{2,0,1:T(8,128)(2,1)}), bf16[128,32,128]{2,0,1:T(8,128)(2,1)S(1)}, u32[]{:S(2)}, u32[]{:S(2)}) async-start(bf16[128,32,128]{2,0,1:T(8,128)(2,1)} %copy.110), calls=%async_computation | async-start | bytes 2097152 | tf_op jit(solution)/shard_map/all_to_all | solution.py:144
  33.1 7.5 %copy-start.11 = (bf16[768,3072]{1,0:T(8,128)(2,1)S(1)}, bf16[768,3072]{1,0:T(8,128)(2,1)}, u32[]{:S(2)}) copy-start(bf16[768,3072]{1,0:T(8,128)(2,1)} %param.26) | copy-start | bytes 14155780
  90.7 87.0 %copy-start.3 = (f32[128,4,8,128]{3,0,1,2:T(8,128)S(1)}, f32[128,4,8,128]{3,0,1,2:T(8,128)}, u32[]{:S(2)}) copy-start(f32[128,4,8,128]{3,0,1,2:T(8,128)} %copy.111) | copy-start | bytes 6291460
  90.7 87.0 %copy-start.14 = (bf16[128,128]{1,0:T(8,128)(2,1)S(1)}, bf16[128,128]{1,0:T(8,128)(2,1)}, u32[]{:S(2)}) copy-start(bf16[128,128]{1,0:T(8,128)(2,1)} %param.20) | copy-start | bytes 98308
  181.1 18.8 %all-to-all-start.1 = ((bf16[512,8,128]{2,1,0:T(8,128)(2,1)}), bf16[512,8,128]{2,1,0:T(8,128)(2,1)S(1)}, u32[]{:S(2)}, u32[]{:S(2)}) async-start(bf16[512,8,128]{2,1,0:T(8,128)(2,1)} %copy.121), calls=%async_computation.1 | async-start | bytes 2097152 | tf_op jit(solution)/shard_map/all_to_all | solution.py:146
  185.2 171.3 %all-gather.7.cloned.1.call-start = ((), (), s32[]{:S(2)}) async-start(), calls=%async_computation.3 | async-start | bytes 26738688 | tf_op jit(solution)/shard_map/all_gather | solution.py:21
  199.9 3.3 copy-start.16
  362.7 2.9 copy-start.6
  362.7 2.9 copy-start.9
  368.6 2.9 copy-start.6
  368.6 2.9 copy-start.9
  374.5 2.9 copy-start.6
  380.5 2.9 copy-start.6
  386.4 2.9 copy-start.6
  392.3 2.9 copy-start.6
  398.2 2.9 copy-start.6
  404.1 2.9 copy-start.6
  410.0 2.9 copy-start.6
  415.9 2.9 copy-start.6
  421.8 2.9 copy-start.6
  427.8 2.9 copy-start.6
  433.7 2.9 copy-start.6
  439.6 2.9 copy-start.6
  445.5 2.9 copy-start.6
  448.9 4.9 %copy-start.1 = (bf16[384,1536]{1,0:T(8,128)(2,1)S(1)}, bf16[384,1536]{1,0:T(8,128)(2,1)}, u32[]{:S(2)}) copy-start(bf16[384,1536]{1,0:T(8,128)(2,1)} %param.25) | copy-start | bytes 3538948
  (47 other events, 68.5 us)
Sparse Core Ops, SparseCore 0:
  26.8 58.5 all-gather.4
  209.9 146.5 all-gather.6
where the time goes:
time: 463 us; the launch traced here: 461 us
  waiting for transfers between devices  134 us (29%)
  local copies, waits for them, and re-layouts  103 us (22%)
  other arithmetic  77.4 us (17%)
  blocking collectives  59.1 us (13%)
  matrix products  49.2 us (11%)
  loops' own time  16.2 us (3%)
  between operations  14.5 us (3%)
  starting transfers between devices  8.01 us (2%)
    all_gather x1, waiting for transfers between devices, combined_all(): gathered = jax.tree.map(lambda a: lax.all_gather(a, axis), part)  98.4 us
    all_gather x2, blocking collectives, combined_all(): gathered = jax.tree.map(lambda a: lax.all_gather(a, axis), part)  46.8 us
    add x15, other arithmetic, combine_parts(): rescale(sum_one, factor_one) + rescale(sum_two, factor_two)  43.6 us
    all_gather x1, waiting for transfers between devices, local(): bias_full = lax.all_gather(partial_bias, 'col', axis=1, tiled=True)  30.4 us
    dynamic_slice x32, local copies, waits for them, and re-layouts, take(): lax.dynamic_index_in_dim(a, source, 0, False)  29.8 us
    dot_general x8, matrix products, one_column(): jnp.einsum('ihd,khd->hik', query_col, key_col, preferred_element_type=jnp...  23.6 us
    another operation x1, loops' own time, attend_columns(): gated = lax.map(one_column, jnp.arange(col_count, dtype=jnp.int32))  15.3 us
    while x135, local copies, waits for them, and re-layouts  13.6 us
  transfers between devices with their start and end apart: 4, of which 3 were waited for; matrix products, arithmetic and copies ran while one was open for 7% of the time, Pallas kernels for 0%

commit v1 on v0

--- a/solution.py
+++ b/solution.py
@@ -140,7 +140,9 @@
         "kiz,zh->hik", normed_tile, tri_bias_weight, preferred_element_type=jnp.float32
     )
     partial_bias = lax.all_gather(local_bias, "row", axis=2, tiled=True)
-    bias_full = lax.all_gather(partial_bias, "col", axis=1, tiled=True)
+    bias_full = jnp.concatenate(
+        lax.all_to_all(jnp.stack([partial_bias] * lax.axis_size("col")), "col", 0, 0), axis=1
+    )
     columns = lax.all_to_all(pair_repr, "row", split_axis=1, concat_axis=0, tiled=True)
     updated = attend_columns(columns, bias_full, tri_weight, tri_output_weight)
     new_tile = lax.all_to_all(updated, "row", split_axis=0, concat_axis=1, tiled=True)

time: 463 us -> 503 us (1.086)
  starting transfers between devices: 8.01 us -> 20.3 us
  local copies, waits for them, and re-layouts: 103 us -> 112 us
  blocking collectives: 59.1 us -> 66.8 us
  waiting for transfers between devices: 134 us -> 141 us
    all_to_all x0 -> x1, waiting for transfers between devices: none -> 37.3 us  [local(): lax.all_to_all(jnp.stack([partial_bias] * lax.axis_size('col')), 'col', 0...]
    all_gather x1 -> x0, waiting for transfers between devices: 30.4 us -> none  [local(): bias_full = lax.all_gather(partial_bias, 'col', axis=1, tiled=True)]
    all_to_all x0 -> x1, starting transfers between devices: none -> 10.5 us  [local(): lax.all_to_all(jnp.stack([partial_bias] * lax.axis_size('col')), 'col', 0...]
    all_gather x2, blocking collectives: 46.8 us -> 56.3 us  [combined_all(): gathered = jax.tree.map(lambda a: lax.all_gather(a, axis), part)]
  transfers between devices with their start and end apart: 4 -> 4, of which waited for: 3 -> 3; matrix products, arithmetic and copies ran while one was open for 7% -> 9% of each run, Pallas kernels for 0% -> 0%
where the time goes in v1:
time: 503 us; the launch traced here: 500 us
  waiting for transfers between devices  141 us (28%)
  local copies, waits for them, and re-layouts  112 us (22%)
  other arithmetic  76.7 us (15%)
  blocking collectives  66.8 us (13%)
  matrix products  51.9 us (10%)
  starting transfers between devices  20.3 us (4%)
  loops' own time  17 us (3%)
  between operations  14.5 us (3%)
    all_gather x1, waiting for transfers between devices, combined_all(): gathered = jax.tree.map(lambda a: lax.all_gather(a, axis), part)  98.8 us
    all_gather x2, blocking collectives, combined_all(): gathered = jax.tree.map(lambda a: lax.all_gather(a, axis), part)  56.3 us
    add x15, other arithmetic, combine_parts(): rescale(sum_one, factor_one) + rescale(sum_two, factor_two)  43.6 us
    all_to_all x1, waiting for transfers between devices, local(): lax.all_to_all(jnp.stack([partial_bias] * lax.axis_size('col')), 'col', 0...  37.3 us
    dynamic_slice x32, local copies, waits for them, and re-layouts, take(): lax.dynamic_index_in_dim(a, source, 0, False)  29.8 us
    dot_general x8, matrix products, one_column(): jnp.einsum('ihd,khd->hik', query_col, key_col, preferred_element_type=jnp...  23.6 us
    another operation x1, loops' own time, attend_columns(): gated = lax.map(one_column, jnp.arange(col_count, dtype=jnp.int32))  16 us
    while x135, local copies, waits for them, and re-layouts  13.6 us
  transfers between devices with their start and end apart: 4, of which 3 were waited for; matrix products, arithmetic and copies ran while one was open for 9% of the time, Pallas kernels for 0%

profile of v1, /device:TPU:1, one launch (start us, length us, event | category | flops | bytes accessed | tf_op | source)
XLA Modules:
  0.0 500.3 jit_solution(797168059240024389)
XLA Ops:
  9.9 6.0 %all-to-all-start = ((bf16[128,32,128]{2,0,1:T(8,128)(2,1)}), bf16[128,32,128]{2,0,1:T(8,128)(2,1)S(1)}, u32[]{:S(2)}, u32[]{:S(2)}) async-start(bf16[128,32,128]{2,0,1:T(8,128)(2,1)} %copy.116), calls=%async_computation | async-start | bytes 2097152 | tf_op jit(solution)/shard_map/all_to_all | solution.py:146
  32.2 10.5 %all_gather.18 = f32[4,32,512]{2,1,0:T(8,128)S(1)} all-gather(f32[4,32,128]{2,1,0:T(8,128)S(1)} %copy.119), channel_id=1, replica_groups=mesh['row'=4,'col'=16,'smp'=2] {'row'}, dimensions={2}, use_global_device_ids=true | all-gather | bytes 327680 | tf_op jit(solution)/shard_map/all_gather | solution.py:142
  45.4 10.5 %all-to-all-start.1 = ((f32[16,4,32,512]{3,2,1,0:T(8,128)}), f32[16,4,32,512]{3,2,1,0:T(8,128)}, u32[]{:S(2)}, u32[]{:S(2)}) async-start(f32[16,4,32,512]{3,2,1,0:T(8,128)} %stack.2), calls=%async_computation.1 | async-start | bytes 8388608 | tf_op jit(solution)/shard_map/all_to_all | solution.py:144
  73.9 37.3 %all-to-all-done.1 = f32[16,4,32,512]{3,2,1,0:T(8,128)} async-done(((f32[16,4,32,512]{3,2,1,0:T(8,128)}), f32[16,4,32,512]{3,2,1,0:T(8,128)}, u32[]{:S(2)}, u32[]{:S(2)}) %all-to-all-start.1) | async-done | bytes 4194336 | tf_op jit(solution)/shard_map/all_to_all | solution.py:144
  111.3 5.0 copy.120
  116.2 5.2 %copy.125 = f32[4,512,512]{1,2,0:T(8,128)} copy(f32[4,512,512]{2,1,0:T(8,128)} %bitcast.197) | data formatting | bytes 8388608 | tf_op jit(solution)/shard_map/while | solution.py:95
  121.5 87.7 %while.29 = (s32[]{:T(128)}, bf16[8,512,128]{1,2,0:T(8,128)(2,1)}, s32[8]{0:T(128)S(1)}, f32[512,8,128]{2,0,1:T(8,128)}, bf16[512,8,128]{2,0,1:T(8,128)(2,1)}, /...) while((s32[]{:T(128)}, bf16[8,512,128]{1,2,0:T(8,128)(2,1)}, ...), condition=%wide.region_7.8_spmd, body=%wide.region_4.7_spmd.sunk | while | flops 140898304 | bytes 20750516 | solution.py:95
  127.4 3.0 fusion.174
  138.4 3.0 fusion.174
  149.4 3.0 fusion.174
  160.3 3.0 fusion.174
  171.3 3.0 fusion.174
  182.2 3.0 fusion.174
  193.2 3.0 fusion.174
  204.1 3.0 fusion.174
  212.5 3.6 all-to-all-start.2
  221.1 2.9 multiply_convert_fusion.2
  225.6 4.8 all-to-all-done.2
  233.7 2.9 convolution_bitcast_fusion
  240.9 35.4 %all-gather = f32[64,16,128]{2,1,0:T(8,128)S(1)} all-gather(f32[4,16,128]{2,1,0:T(8,128)S(1)} %get-tuple-element.335), channel_id=2, replica_groups=mesh['row'=4,'col'=16,'smp'=2] {'col'}, dimensions={0}, use_global_device_ids=true | all-gather | bytes 557056 | tf_op jit(solution)/shard_map/all_gather | solution.py:21
  276.6 20.9 %all-gather.1 = f32[64,16,128]{2,1,0:T(8,128)S(1)} all-gather(f32[4,16,128]{2,1,0:T(8,128)S(1)} %fusion.85), channel_id=3, replica_groups=mesh['row'=4,'col'=16,'smp'=2] {'col'}, dimensions={0}, use_global_device_ids=true | all-gather | bytes 557056 | tf_op jit(solution)/shard_map/all_gather | solution.py:21
  297.5 98.8 %all-gather.4.cloned.1.call-done = f32[16,4,128,768]{3,2,1,0:T(8,128)} async-done(((f32[1,4,128,768]{3,2,1,0:T(8,128)}), f32[16,4,128,768]{3,2,1,0:T(8,128)}) %all-gather.4.cloned.1.call-update) | async-done | bytes 25165840 | tf_op jit(solution)/shard_map/all_gather | solution.py:21
  399.5 88.7 %while.30 = (s32[]{:T(128)}, f32[4,16,128]{2,1,0:T(8,128)S(1)}, f32[4,16,128]{2,1,0:T(8,128)S(1)}, f32[4,128,768]{1,2,0:T(8,128)}, f32[16,4,16,128]{3,2,1,0:T(8,...) while((s32[]{:T(128)}, f32[4,16,128]{2,1,0:T(8,128)S(1)}, ...), condition=%wide.region_21.22_spmd, body=%wide.region_20.21_spmd.sunk | while | flops 1236997 | bytes 19890436 | solution.py:26
  414.4 2.9 fusion.179
  420.3 2.9 fusion.179
  426.2 2.9 fusion.179
  432.1 2.9 fusion.179
  438.0 2.9 fusion.179
  443.9 2.9 fusion.179
  449.8 2.9 fusion.179
  455.7 2.9 fusion.179
  461.7 2.9 fusion.179
  (400 shorter events, 175.2 us)
Async XLA Ops:
  7.2 50.3 %copy-start = (bf16[384,1536]{1,0:T(8,128)(2,1)S(1)}, bf16[384,1536]{1,0:T(8,128)(2,1)}, u32[]{:S(2)}) copy-start(bf16[384,1536]{1,0:T(8,128)(2,1)} %param.25) | copy-start | bytes 3538948
  7.2 8.8 %copy-start.2 = (bf16[128,32,128]{2,1,0:T(8,128)(2,1)S(1)}, bf16[128,32,128]{2,1,0:T(8,128)(2,1)}, u32[]{:S(2)}) copy-start(bf16[128,32,128]{2,1,0:T(8,128)(2,1)} %param.17) | copy-start | bytes 3145732
  9.9 11.3 %copy-start.18 = (s32[4]{0:T(128)S(1)}, s32[4]{0:T(128)}, u32[]{:S(2)}) copy-start(s32[4]{0:T(128)} %param.22) | copy-start | bytes 52
  9.9 33.0 %all-to-all-start = ((bf16[128,32,128]{2,0,1:T(8,128)(2,1)}), bf16[128,32,128]{2,0,1:T(8,128)(2,1)S(1)}, u32[]{:S(2)}, u32[]{:S(2)}) async-start(bf16[128,32,128]{2,0,1:T(8,128)(2,1)} %copy.116), calls=%async_computation | async-start | bytes 2097152 | tf_op jit(solution)/shard_map/all_to_all | solution.py:146
  15.9 10.5 %copy-start.17 = (bf16[128,4]{0,1:T(4,128)(2,1)S(1)}, bf16[128,4]{0,1:T(4,128)(2,1)}, u32[]{:S(2)}) copy-start(bf16[128,4]{0,1:T(4,128)(2,1)} %param.19) | copy-start | bytes 3076
  45.4 65.8 %all-to-all-start.1 = ((f32[16,4,32,512]{3,2,1,0:T(8,128)}), f32[16,4,32,512]{3,2,1,0:T(8,128)}, u32[]{:S(2)}, u32[]{:S(2)}) async-start(f32[16,4,32,512]{3,2,1,0:T(8,128)} %stack.2), calls=%async_computation.1 | async-start | bytes 8388608 | tf_op jit(solution)/shard_map/all_to_all | solution.py:144
  121.5 87.7 %copy-start.3 = (f32[128,4,8,128]{3,0,1,2:T(8,128)S(1)}, f32[128,4,8,128]{3,0,1,2:T(8,128)}, u32[]{:S(2)}) copy-start(f32[128,4,8,128]{3,0,1,2:T(8,128)} %copy.117) | copy-start | bytes 6291460
  121.5 87.7 %copy-start.13 = (bf16[128,128]{1,0:T(8,128)(2,1)S(1)}, bf16[128,128]{1,0:T(8,128)(2,1)}, u32[]{:S(2)}) copy-start(bf16[128,128]{1,0:T(8,128)(2,1)} %param.20) | copy-start | bytes 98308
  210.8 5.5 %copy-start.11 = (bf16[4,32,768]{2,1,0:T(8,128)(2,1)S(1)}, bf16[4,32,768]{2,1,0:T(8,128)(2,1)}, u32[]{:S(2)}) copy-start(bf16[4,32,768]{2,1,0:T(8,128)(2,1)} %get-tuple-element.327) | copy-start | bytes 589828
  210.9 6.1 %copy-start.10 = (bf16[4,32,768]{2,1,0:T(8,128)(2,1)S(1)}, bf16[4,32,768]{2,1,0:T(8,128)(2,1)}, u32[]{:S(2)}) copy-start(bf16[4,32,768]{2,1,0:T(8,128)(2,1)} %get-tuple-element.328) | copy-start | bytes 589828
  212.5 17.8 %all-to-all-start.2 = ((bf16[512,8,128]{2,1,0:T(8,128)(2,1)}), bf16[512,8,128]{2,1,0:T(8,128)(2,1)S(1)}, u32[]{:S(2)}, u32[]{:S(2)}) async-start(bf16[512,8,128]{2,1,0:T(8,128)(2,1)} %copy.127), calls=%async_computation.2 | async-start | bytes 2097152 | tf_op jit(solution)/shard_map/all_to_all | solution.py:148
  216.1 180.2 %all-gather.4.cloned.1.call-start = ((), (), s32[]{:S(2)}) async-start(), calls=%async_computation.3 | async-start | bytes 26738688 | tf_op jit(solution)/shard_map/all_gather | solution.py:21
  230.4 3.3 copy-start.16
  402.5 2.9 copy-start.5
  402.5 2.9 copy-start.8
  408.4 2.9 copy-start.5
  408.4 2.9 copy-start.8
  414.3 2.9 copy-start.5
  414.4 2.9 copy-start.8
  420.3 2.9 copy-start.5
  426.2 2.9 copy-start.5
  432.1 2.9 copy-start.5
  438.0 2.9 copy-start.5
  443.9 2.9 copy-start.5
  449.8 2.9 copy-start.5
  455.7 2.9 copy-start.5
  461.6 2.9 copy-start.5
  467.5 2.9 copy-start.5
  473.5 2.9 copy-start.5
  479.4 2.9 copy-start.5
  485.3 2.9 copy-start.5
  488.6 4.9 copy-start.1
  (47 other events, 69.1 us)
Sparse Core Ops, SparseCore 0:
  239.8 156.4 all-gather.3
